TPU v7x, 32 devices: a whole 2x2x4 slice. The times are simulated.
32 devices in a mesh: gz: 8 (over z, y), xy: 4 (over x, core).
Axes of the slice: x: 2, y: 2, z: 4, core: 2. Of those that a mesh axis runs over, the one named last changes fastest.
Arguments:
- up_source: bfloat16 [8, 2, 32, 1024], P('gz', None, None, 'xy'), may hold values from -6 to 6
- down_source: bfloat16 [8, 2, 32, 1024], P('gz', None, None, 'xy'), may hold values from -6 to 6
- source_layer: int32 [32], replicated, may hold values from 0 to 7, as said below
- u_factor: bfloat16 [8, 4, 4, 2, 128, 256], P('gz', 'xy'), may hold values from -0.15625 to 0.15625
- v_factor: bfloat16 [8, 4, 4, 2, 128, 256], P('gz', 'xy'), may hold values from -0.25 to 0.25
- block_rank: int32 [8, 4, 4], P('gz', 'xy'), may hold values from 1 to 4
Outputs:
- up_trace: bfloat16 [8, 2, 32, 1024], P('gz', None, None, 'xy')
- down_trace: bfloat16 [8, 2, 32, 1024], P('gz', None, None, 'xy')
Inputs may be any that keep to these rules, and one draw needn't show every extreme that they name: `source_layer`: the index of the layer slab in which source s lies; source 0 lies in slab 0 and source 1 in slab 8 - 1. `block_rank`: block (i, j) of interface l has rank 32 times this number.
All inputs are finite; a program needn't handle non-finite values.
Results may differ from a plain program's by a relative error of at most 0.007.
Values may be sent and summed in bfloat16 or wider, within the bound.
A program may use at most 64 MiB of HBM per device.

v0:
```python
import jax
import jax.numpy as jnp
from jax import lax
from jax.sharding import PartitionSpec as P

STEPS = 3


def from_behind(block, axis, distance):
    devices = range(lax.axis_size(axis))
    route = [(i - distance, i) for i in devices if i - distance in devices]
    return lax.ppermute(block, axis, route)


def complex_parts(product):
    real = product[..., 0, :, 0, :] - product[..., 1, :, 1, :]
    imag = product[..., 0, :, 1, :] + product[..., 1, :, 0, :]
    return jnp.stack([real, imag], axis=-3)


def advance(up_part, down_part, active_up, active_down, u_layer, v_layer, keep_rank, v_columns):
    sources = up_part.shape[1]
    own_rows = u_layer.shape[0]
    blocks = u_layer.shape[1]
    width = u_layer.shape[-1]
    gathered = lax.all_gather(up_part, "xy", axis=2, tiled=True)
    pieces = gathered.reshape(2, sources, blocks, width)
    up_coef = complex_parts(
        jnp.einsum("asjb,ijcrb->ijascr", pieces, v_layer, preferred_element_type=jnp.float32)
    )
    up_coef = jnp.where(keep_rank[:, :, None, None, :], up_coef, 0.0).astype(jnp.bfloat16)
    forward = complex_parts(
        jnp.einsum("ijasr,ijcrb->iascb", up_coef, u_layer, preferred_element_type=jnp.float32)
    )
    forward = jnp.transpose(forward, (1, 2, 0, 3)).reshape(2, sources, own_rows * width)
    arrived = from_behind(forward, "gz", 1)
    new_up = (active_up.astype(jnp.float32) + arrived).astype(jnp.bfloat16)
    upper = from_behind(down_part, "gz", -1)
    upper_blocks = upper.reshape(2, sources, own_rows, width)
    down_coef = complex_parts(
        jnp.einsum("asib,ijcrb->ijascr", upper_blocks, u_layer, preferred_element_type=jnp.float32)
    )
    down_coef = jnp.where(keep_rank[:, :, None, None, :], down_coef, 0.0).astype(jnp.bfloat16)
    column_coef = lax.all_to_all(down_coef, "xy", split_axis=1, concat_axis=0, tiled=True)
    summed = complex_parts(
        jnp.einsum("ijasr,ijcrb->jascb", column_coef, v_columns, preferred_element_type=jnp.float32)
    )
    backward = jnp.transpose(summed, (1, 2, 0, 3)).reshape(2, sources, own_rows * width)
    new_down = (active_down.astype(jnp.float32) + backward).astype(jnp.bfloat16)
    return (new_up, new_down)


def on_device(up_source, down_source, source_layer, u_factor, v_factor, block_rank):
    layer_index = lax.axis_index("gz")
    up_mask = (layer_index >= source_layer)[None, :, None]
    down_mask = (layer_index <= source_layer)[None, :, None]
    active_up = jnp.where(up_mask, up_source[0], jnp.zeros_like(up_source[0]))
    active_down = jnp.where(down_mask, down_source[0], jnp.zeros_like(down_source[0]))
    u_layer = u_factor[0]
    v_layer = v_factor[0]
    rank_units = block_rank[0]
    max_rank = u_layer.shape[-2]
    keep_rank = (
        jnp.arange(max_rank, dtype=jnp.int32)[None, None, :]
        < max_rank // 4 * rank_units[:, :, None]
    )
    v_columns = lax.all_to_all(v_layer, "xy", split_axis=1, concat_axis=0, tiled=True)
    up_trace = active_up
    down_trace = active_down
    for sweep_index in range(STEPS):
        up_trace, down_trace = advance(
            up_trace, down_trace, active_up, active_down, u_layer, v_layer, keep_rank, v_columns
        )
    return (up_trace[None], down_trace[None])


def solution(mesh):
    in_specs = (
        P("gz", None, None, "xy"),
        P("gz", None, None, "xy"),
        P(),
        P("gz", "xy", None, None, None, None),
        P("gz", "xy", None, None, None, None),
        P("gz", "xy", None),
    )
    out_specs = (P("gz", None, None, "xy"), P("gz", None, None, "xy"))
    return jax.shard_map(
        on_device, mesh=mesh, in_specs=in_specs, out_specs=out_specs, check_vma=False
    )
```

profile of v0, /device:TPU:0, one launch (start us, length us, event | category | flops | bytes accessed | tf_op | source)
XLA Modules:
  0.0 86.9 jit_solution(7317015157043258093)
XLA Ops:
  0.7 0.7 copy-done.3
  1.4 0.8 bitcast_select_fusion
  2.2 1.3 %collective-permute-start.3 = (bf16[2,32,256]{2,1,0:T(8,128)(2,1)S(1)}, bf16[2,32,256]{2,1,0:T(8,128)(2,1)S(1)}, u32[]{:S(2)}, u32[]{:S(2)}) collective-permute-start(bf16[2,32,256]{2,1,0:T(8,128)(2,1)S(1)} %bitcast_select_fusion), channel_id=1, source_target_pairs={{4,0},{8,4},{12,8},{16,12},{20,16},{24,20},{28,24},{5,1},{9,5},{13... | collective-permute-start | bytes 98312 | tf_op jit(solution)/shard_map/ppermute | solution.py:12
  3.6 6.5 %all_gather.9 = bf16[2,32,1024]{2,1,0:T(8,128)(2,1)S(1)} all-gather(bf16[2,32,256]{2,1,0:T(8,128)(2,1)S(1)} %bitcast_select_fusion.1), channel_id=1, replica_groups=mesh['gz'=8,'xy'=4] {'xy'}, dimensions={2}, use_global_device_ids=true | all-gather | bytes 163840 | tf_op jit(solution)/shard_map/all_gather | solution.py:26
  10.2 1.3 %convolution_bitcast_fusion.5 = f32[1,4,2,32,2,128]{5,3,4,2,1,0:T(8,128)S(1)} fusion(bf16[1,1,4,2,128,256]{5,4,3,2,1,0:T(8,128)(2,1)} %param.10, bf16[2,32,4,256,1]{3,2,1,0,4:T(4,128)(2,1)S(1)} %bitcast.274), kind=kOutput, calls=%fused_computation.5 | convolution fusion | flops 33554432 | bytes 917504 | tf_op jit(solution)/shard_map/asjb,ijcrb->ijascr/dot_general | solution.py:29
  12.5 4.5 %collective-permute-start = (f32[2,32,256]{2,1,0:T(8,128)S(1)}, f32[2,32,256]{2,1,0:T(8,128)S(1)}, u32[]{:S(2)}, u32[]{:S(2)}) collective-permute-start(f32[2,32,256]{2,1,0:T(8,128)S(1)} %maximum_bitcast_fusion), channel_id=1, source_target_pairs={{0,4},{4,8},{8,12},{12,16},{16,20},{20,24},{24,28},{1,5},{5,9},{9,... | collective-permute-start | bytes 196616 | tf_op jit(solution)/shard_map/ppermute | solution.py:12
  17.4 1.6 %collective-permute-done = f32[2,32,256]{2,1,0:T(8,128)S(1)} collective-permute-done((f32[2,32,256]{2,1,0:T(8,128)S(1)}, f32[2,32,256]{2,1,0:T(8,128)S(1)}, u32[]{:S(2)}, u32[]{:S(2)}) %collective-permute-start) | collective-permute-done | bytes 65568 | tf_op jit(solution)/shard_map/ppermute | solution.py:12
  19.0 5.4 %all_gather.10 = bf16[2,32,1024]{2,1,0:T(8,128)(2,1)S(1)} all-gather(bf16[2,32,256]{2,1,0:T(8,128)(2,1)S(1)} %fusion.33), channel_id=1, replica_groups=mesh['gz'=8,'xy'=4] {'xy'}, dimensions={2}, use_global_device_ids=true | all-gather | bytes 163840 | tf_op jit(solution)/shard_map/all_gather | solution.py:26
  24.5 1.3 %convolution_bitcast_fusion.4 = f32[1,4,2,32,2,128]{5,3,1,4,2,0:T(8,128)S(1)} fusion(bf16[2,32,4,256,1]{3,2,1,0,4:T(4,128)(2,1)S(1)} %bitcast.275, bf16[1,1,4,2,128,256]{5,4,3,2,1,0:T(8,128)(2,1)} %param.10), kind=kOutput, calls=%fused_computation.4 | convolution fusion | flops 33554432 | bytes 917504 | tf_op jit(solution)/shard_map/asjb,ijcrb->ijascr/dot_general | solution.py:29
  26.1 4.7 %collective-permute-start.1 = (f32[2,32,256]{2,1,0:T(8,128)S(1)}, f32[2,32,256]{2,1,0:T(8,128)S(1)}, u32[]{:S(2)}, u32[]{:S(2)}) collective-permute-start(f32[2,32,256]{2,1,0:T(8,128)S(1)} %maximum_bitcast_fusion.1), channel_id=1, source_target_pairs={{0,4},{4,8},{8,12},{12,16},{16,20},{20,24},{24,28},{1,5},{5,9},{9,... | collective-permute-start | bytes 196616 | tf_op jit(solution)/shard_map/ppermute | solution.py:12
  31.4 3.3 %all-to-all-start = ((bf16[1,4,2,32,128]{4,3,2,0,1:T(8,128)(2,1)}), bf16[1,4,2,32,128]{4,3,2,0,1:T(8,128)(2,1)S(1)}, u32[]{:S(2)}, u32[]{:S(2)}) async-start(bf16[1,4,2,32,128]{4,3,2,0,1:T(8,128)(2,1)} %copy.49), calls=%async_computation | async-start | bytes 131072 | tf_op jit(solution)/shard_map/all_to_all | solution.py:44
  34.8 4.0 %all-to-all-done = bf16[1,4,2,32,128]{4,3,2,0,1:T(8,128)(2,1)S(1)} async-done(((bf16[1,4,2,32,128]{4,3,2,0,1:T(8,128)(2,1)}), bf16[1,4,2,32,128]{4,3,2,0,1:T(8,128)(2,1)S(1)}, u32[]{:S(2)}, u32[]{:S(2)}) %all-to-all-start) | async-done | bytes 65568 | tf_op jit(solution)/shard_map/all_to_all | solution.py:44
  38.8 3.5 %all-to-all-start.1 = ((bf16[1,4,2,128,256]{4,3,2,0,1:T(8,128)(2,1)}), bf16[1,4,2,128,256]{4,3,2,0,1:T(8,128)(2,1)S(1)}, u32[]{:S(2)}, u32[]{:S(2)}) async-start(bf16[1,4,2,128,256]{4,3,2,0,1:T(8,128)(2,1)} %bitcast.74), calls=%async_computation.1 | async-start | bytes 1048576 | tf_op jit(solution)/shard_map/all_to_all | solution.py:67
  42.3 10.3 %all_gather.11 = bf16[2,32,1024]{2,1,0:T(8,128)(2,1)S(1)} all-gather(bf16[2,32,256]{2,1,0:T(8,128)(2,1)S(1)} %fusion.34), channel_id=1, replica_groups=mesh['gz'=8,'xy'=4] {'xy'}, dimensions={2}, use_global_device_ids=true | all-gather | bytes 163840 | tf_op jit(solution)/shard_map/all_gather | solution.py:26
  52.7 1.3 %convolution_bitcast_fusion.3 = f32[1,4,2,32,2,128]{5,3,1,4,2,0:T(8,128)S(1)} fusion(bf16[2,32,4,256,1]{3,2,1,0,4:T(4,128)(2,1)S(1)} %bitcast.276, bf16[1,1,4,2,128,256]{5,4,3,2,1,0:T(8,128)(2,1)} %param.10), kind=kOutput, calls=%fused_computation.3 | convolution fusion | flops 33554432 | bytes 917504 | tf_op jit(solution)/shard_map/asjb,ijcrb->ijascr/dot_general | solution.py:29
  54.3 0.7 copy-done.2
  55.1 1.3 %collective-permute-start.4 = (bf16[2,32,256]{2,1,0:T(8,128)(2,1)S(1)}, bf16[2,32,256]{2,1,0:T(8,128)(2,1)S(1)}, u32[]{:S(2)}, u32[]{:S(2)}) collective-permute-start(bf16[2,32,256]{2,1,0:T(8,128)(2,1)S(1)} %fusion.31), channel_id=1, source_target_pairs={{4,0},{8,4},{12,8},{16,12},{20,16},{24,20},{28,24},{5,1},{9,5},{13... | collective-permute-start | bytes 98312 | tf_op jit(solution)/shard_map/ppermute | solution.py:12
  56.6 5.6 %collective-permute-done.4 = bf16[2,32,256]{2,1,0:T(8,128)(2,1)S(1)} collective-permute-done((bf16[2,32,256]{2,1,0:T(8,128)(2,1)S(1)}, bf16[2,32,256]{2,1,0:T(8,128)(2,1)S(1)}, u32[]{:S(2)}, u32[]{:S(2)}) %collective-permute-start.4) | collective-permute-done | bytes 32800 | tf_op jit(solution)/shard_map/ppermute | solution.py:12
  63.2 3.3 %all-to-all-start.2 = ((bf16[1,4,2,32,128]{4,3,2,0,1:T(8,128)(2,1)}), bf16[1,4,2,32,128]{4,3,2,0,1:T(8,128)(2,1)S(1)}, u32[]{:S(2)}, u32[]{:S(2)}) async-start(bf16[1,4,2,32,128]{4,3,2,0,1:T(8,128)(2,1)} %copy.53), calls=%async_computation.2 | async-start | bytes 131072 | tf_op jit(solution)/shard_map/all_to_all | solution.py:44
  66.5 4.1 %all-to-all-done.2 = bf16[1,4,2,32,128]{4,3,2,0,1:T(8,128)(2,1)S(1)} async-done(((bf16[1,4,2,32,128]{4,3,2,0,1:T(8,128)(2,1)}), bf16[1,4,2,32,128]{4,3,2,0,1:T(8,128)(2,1)S(1)}, u32[]{:S(2)}, u32[]{:S(2)}) %all-to-all-start.2) | async-done | bytes 65568 | tf_op jit(solution)/shard_map/all_to_all | solution.py:44
  70.9 1.3 %collective-permute-start.5 = (bf16[2,32,256]{2,1,0:T(8,128)(2,1)S(1)}, bf16[2,32,256]{2,1,0:T(8,128)(2,1)S(1)}, u32[]{:S(2)}, u32[]{:S(2)}) collective-permute-start(bf16[2,32,256]{2,1,0:T(8,128)(2,1)S(1)} %fusion.32), channel_id=1, source_target_pairs={{4,0},{8,4},{12,8},{16,12},{20,16},{24,20},{28,24},{5,1},{9,5},{13... | collective-permute-start | bytes 98312 | tf_op jit(solution)/shard_map/ppermute | solution.py:12
  72.2 5.5 %collective-permute-start.2 = (f32[2,32,256]{2,1,0:T(8,128)S(1)}, f32[2,32,256]{2,1,0:T(8,128)S(1)}, u32[]{:S(2)}, u32[]{:S(2)}) collective-permute-start(f32[2,32,256]{2,1,0:T(8,128)S(1)} %maximum_bitcast_fusion.2), channel_id=1, source_target_pairs={{0,4},{4,8},{8,12},{12,16},{16,20},{20,24},{24,28},{1,5},{5,9},{9,... | collective-permute-start | bytes 196616 | tf_op jit(solution)/shard_map/ppermute | solution.py:12
  78.6 3.3 %all-to-all-start.3 = ((bf16[1,4,2,32,128]{4,3,2,0,1:T(8,128)(2,1)}), bf16[1,4,2,32,128]{4,3,2,0,1:T(8,128)(2,1)S(1)}, u32[]{:S(2)}, u32[]{:S(2)}) async-start(bf16[1,4,2,32,128]{4,3,2,0,1:T(8,128)(2,1)} %copy.56), calls=%async_computation.3 | async-start | bytes 131072 | tf_op jit(solution)/shard_map/all_to_all | solution.py:44
  82.6 3.4 %all-to-all-done.3 = bf16[1,4,2,32,128]{4,3,2,0,1:T(8,128)(2,1)S(1)} async-done(((bf16[1,4,2,32,128]{4,3,2,0,1:T(8,128)(2,1)}), bf16[1,4,2,32,128]{4,3,2,0,1:T(8,128)(2,1)S(1)}, u32[]{:S(2)}, u32[]{:S(2)}) %all-to-all-start.3) | async-done | bytes 65568 | tf_op jit(solution)/shard_map/all_to_all | solution.py:44
  (58 shorter events, 7.0 us)
Async XLA Ops:
  0.6 11.6 %copy-start = (bf16[1,1,4,2,128,256]{5,4,3,2,1,0:T(8,128)(2,1)S(1)}, bf16[1,1,4,2,128,256]{5,4,3,2,1,0:T(8,128)(2,1)}, u32[]{:S(2)}) copy-start(bf16[1,1,4,2,128,256]{5,4,3,2,1,0:T(8,128)(2,1)} %param.9) | copy-start | bytes 1572868
  0.6 0.7 copy-start.3
  1.4 2.1 %copy-start.1 = (bf16[1,2,32,256]{3,2,1,0:T(8,128)(2,1)S(1)}, bf16[1,2,32,256]{3,2,1,0:T(8,128)(2,1)}, u32[]{:S(2)}) copy-start(bf16[1,2,32,256]{3,2,1,0:T(8,128)(2,1)} %param.6) | copy-start | bytes 98308
  2.2 14.8 %collective-permute-start.3 = (bf16[2,32,256]{2,1,0:T(8,128)(2,1)S(1)}, bf16[2,32,256]{2,1,0:T(8,128)(2,1)S(1)}, u32[]{:S(2)}, u32[]{:S(2)}) collective-permute-start(bf16[2,32,256]{2,1,0:T(8,128)(2,1)S(1)} %bitcast_select_fusion), channel_id=1, source_target_pairs={{4,0},{8,4},{12,8},{16,12},{20,16},{24,20},{28,24},{5,1},{9,5},{13... | collective-permute-start | bytes 98312 | tf_op jit(solution)/shard_map/ppermute | solution.py:12
  11.5 0.7 copy-start.4
  12.5 6.4 %collective-permute-start = (f32[2,32,256]{2,1,0:T(8,128)S(1)}, f32[2,32,256]{2,1,0:T(8,128)S(1)}, u32[]{:S(2)}, u32[]{:S(2)}) collective-permute-start(f32[2,32,256]{2,1,0:T(8,128)S(1)} %maximum_bitcast_fusion), channel_id=1, source_target_pairs={{0,4},{4,8},{8,12},{12,16},{16,20},{20,24},{24,28},{1,5},{5,9},{9,... | collective-permute-start | bytes 196616 | tf_op jit(solution)/shard_map/ppermute | solution.py:12
  26.1 8.7 %collective-permute-start.1 = (f32[2,32,256]{2,1,0:T(8,128)S(1)}, f32[2,32,256]{2,1,0:T(8,128)S(1)}, u32[]{:S(2)}, u32[]{:S(2)}) collective-permute-start(f32[2,32,256]{2,1,0:T(8,128)S(1)} %maximum_bitcast_fusion.1), channel_id=1, source_target_pairs={{0,4},{4,8},{8,12},{12,16},{16,20},{20,24},{24,28},{1,5},{5,9},{9,... | collective-permute-start | bytes 196616 | tf_op jit(solution)/shard_map/ppermute | solution.py:12
  31.4 7.4 %all-to-all-start = ((bf16[1,4,2,32,128]{4,3,2,0,1:T(8,128)(2,1)}), bf16[1,4,2,32,128]{4,3,2,0,1:T(8,128)(2,1)S(1)}, u32[]{:S(2)}, u32[]{:S(2)}) async-start(bf16[1,4,2,32,128]{4,3,2,0,1:T(8,128)(2,1)} %copy.49), calls=%async_computation | async-start | bytes 131072 | tf_op jit(solution)/shard_map/all_to_all | solution.py:44
  38.8 15.2 %all-to-all-start.1 = ((bf16[1,4,2,128,256]{4,3,2,0,1:T(8,128)(2,1)}), bf16[1,4,2,128,256]{4,3,2,0,1:T(8,128)(2,1)S(1)}, u32[]{:S(2)}, u32[]{:S(2)}) async-start(bf16[1,4,2,128,256]{4,3,2,0,1:T(8,128)(2,1)} %bitcast.74), calls=%async_computation.1 | async-start | bytes 1048576 | tf_op jit(solution)/shard_map/all_to_all | solution.py:67
  54.3 0.8 copy-start.2
  55.1 7.1 %collective-permute-start.4 = (bf16[2,32,256]{2,1,0:T(8,128)(2,1)S(1)}, bf16[2,32,256]{2,1,0:T(8,128)(2,1)S(1)}, u32[]{:S(2)}, u32[]{:S(2)}) collective-permute-start(bf16[2,32,256]{2,1,0:T(8,128)(2,1)S(1)} %fusion.31), channel_id=1, source_target_pairs={{4,0},{8,4},{12,8},{16,12},{20,16},{24,20},{28,24},{5,1},{9,5},{13... | collective-permute-start | bytes 98312 | tf_op jit(solution)/shard_map/ppermute | solution.py:12
  63.2 7.4 %all-to-all-start.2 = ((bf16[1,4,2,32,128]{4,3,2,0,1:T(8,128)(2,1)}), bf16[1,4,2,32,128]{4,3,2,0,1:T(8,128)(2,1)S(1)}, u32[]{:S(2)}, u32[]{:S(2)}) async-start(bf16[1,4,2,32,128]{4,3,2,0,1:T(8,128)(2,1)} %copy.53), calls=%async_computation.2 | async-start | bytes 131072 | tf_op jit(solution)/shard_map/all_to_all | solution.py:44
  70.9 6.8 %collective-permute-start.5 = (bf16[2,32,256]{2,1,0:T(8,128)(2,1)S(1)}, bf16[2,32,256]{2,1,0:T(8,128)(2,1)S(1)}, u32[]{:S(2)}, u32[]{:S(2)}) collective-permute-start(bf16[2,32,256]{2,1,0:T(8,128)(2,1)S(1)} %fusion.32), channel_id=1, source_target_pairs={{4,0},{8,4},{12,8},{16,12},{20,16},{24,20},{28,24},{5,1},{9,5},{13... | collective-permute-start | bytes 98312 | tf_op jit(solution)/shard_map/ppermute | solution.py:12
  72.2 9.7 %collective-permute-start.2 = (f32[2,32,256]{2,1,0:T(8,128)S(1)}, f32[2,32,256]{2,1,0:T(8,128)S(1)}, u32[]{:S(2)}, u32[]{:S(2)}) collective-permute-start(f32[2,32,256]{2,1,0:T(8,128)S(1)} %maximum_bitcast_fusion.2), channel_id=1, source_target_pairs={{0,4},{4,8},{8,12},{12,16},{16,20},{20,24},{24,28},{1,5},{5,9},{9,... | collective-permute-start | bytes 196616 | tf_op jit(solution)/shard_map/ppermute | solution.py:12
  78.6 7.4 %all-to-all-start.3 = ((bf16[1,4,2,32,128]{4,3,2,0,1:T(8,128)(2,1)}), bf16[1,4,2,32,128]{4,3,2,0,1:T(8,128)(2,1)S(1)}, u32[]{:S(2)}, u32[]{:S(2)}) async-start(bf16[1,4,2,32,128]{4,3,2,0,1:T(8,128)(2,1)} %copy.56), calls=%async_computation.3 | async-start | bytes 131072 | tf_op jit(solution)/shard_map/all_to_all | solution.py:44
where the time goes:
time: 87.8 us; the launch traced here: 86.9 us
  starting transfers between devices  31.9 us (36%)
  blocking collectives  22.2 us (25%)
  waiting for transfers between devices  18.6 us (21%)
  matrix products  6 us (7%)
  local copies, waits for them, and re-layouts  4.16 us (5%)
  other arithmetic  3 us (3%)
  between operations  1.02 us (1%)
    all_gather x3, blocking collectives, advance(): gathered = lax.all_gather(up_part, 'xy', axis=2, tiled=True)  22.2 us
    ppermute x6, starting transfers between devices, from_behind(): return lax.ppermute(block, axis, route)  18.5 us
    all_to_all x3, waiting for transfers between devices, advance(): lax.all_to_all(down_coef, 'xy', split_axis=1, concat_axis=0, tiled=True)  11.4 us
    all_to_all x3, starting transfers between devices, advance(): lax.all_to_all(down_coef, 'xy', split_axis=1, concat_axis=0, tiled=True)  9.85 us
    ppermute x6, waiting for transfers between devices, from_behind(): return lax.ppermute(block, axis, route)  7.18 us
    dot_general x3, matrix products, advance(): jnp.einsum('asjb,ijcrb->ijascr', pieces, v_layer, preferred_element_type=...  3.95 us
    all_to_all x1, starting transfers between devices, on_device(): lax.all_to_all(v_layer, 'xy', split_axis=1, concat_axis=0, tiled=True)  3.47 us
    unnamed x10, local copies, waits for them, and re-layouts  2.08 us
  transfers between devices with their start and end apart: 10, of which 5 were waited for; matrix products, arithmetic and copies ran while one was open for 7% of the time, Pallas kernels for 0%

commit v1 on v0

v1 whole, which is shorter than its diff:
```python
import functools

import jax
import jax.numpy as jnp
from jax import lax
from jax.experimental import pallas as pl
from jax.experimental.pallas import tpu as pltpu
from jax.sharding import PartitionSpec as P

STEPS = 3
MESH = pl.DeviceIdType.MESH


def kernel(
    layers, n, up_ref, down_ref, layer_ref, u_hbm, v_hbm, rank_ref, up_out, down_out,
    u_mem, v_mem, up_all, up_send, up_next, up_last, own_down, down_first, part, part_send,
    load_sem, up_ssem, up_rsem, next_ssem, next_rsem, last_ssem, last_rsem,
    first_ssem, first_rsem, part_ssem, part_rsem,
):
    layer = lax.axis_index("gz")
    me = lax.axis_index("xy")
    has_above = layer < layers - 1
    has_below = layer > 0
    rows, width = up_send.shape[1:]
    sources = rows // 2
    max_rank = u_mem.shape[2]
    others = [lax.rem(me + k, n) for k in range(n)]

    def remote(src, dst, ssem, rsem, to_layer, to_block):
        return pltpu.make_async_remote_copy(
            src_ref=src, dst_ref=dst, send_sem=ssem, recv_sem=rsem,
            device_id={"gz": to_layer, "xy": to_block}, device_id_type=MESH,
        )

    load_u = pltpu.make_async_copy(u_hbm.at[0, 0], u_mem, load_sem.at[0])
    load_v = pltpu.make_async_copy(v_hbm.at[0, 0], v_mem, load_sem.at[1])
    load_v.start()
    load_u.start()

    barrier = pltpu.get_barrier_semaphore()

    def greet(to_layer, to_block):
        pl.semaphore_signal(
            barrier, inc=1, device_id={"gz": to_layer, "xy": to_block}, device_id_type=MESH
        )

    for k in range(1, n):
        greet(layer, others[k])

    @pl.when(has_above)
    def _():
        for k in range(n):
            greet(layer + 1, others[k])

    @pl.when(has_below)
    def _():
        for k in range(n):
            greet(layer - 1, others[k])

    square = (sources, sources)
    diagonal = lax.broadcasted_iota(jnp.int32, square, 0) == lax.broadcasted_iota(jnp.int32, square, 1)
    source_layer = jnp.sum(
        jnp.where(diagonal, jnp.broadcast_to(layer_ref[...], square), 0), axis=1, keepdims=True
    )
    source_layer = jnp.broadcast_to(jnp.concatenate([source_layer, source_layer], axis=0), (rows, width))
    up_own = jnp.where(
        layer >= source_layer, up_ref[0].reshape(rows, width).astype(jnp.float32), 0.0
    ).astype(jnp.bfloat16)
    down_own = jnp.where(
        layer <= source_layer, down_ref[0].reshape(rows, width).astype(jnp.float32), 0.0
    ).astype(jnp.bfloat16)
    up_all[0, me] = up_own
    own_down[...] = down_own

    @pl.when(jnp.logical_not(has_above))
    def _():
        up_next[...] = jnp.zeros_like(up_next)
        down_first[...] = jnp.zeros_like(down_first)
        part[0] = jnp.zeros_like(part[0])
        part[1] = jnp.zeros_like(part[1])

    peers = n - 1 + jnp.where(has_above, n, 0) + jnp.where(has_below, n, 0)
    pl.semaphore_wait(barrier, peers)

    def gather(k):
        return remote(
            up_all.at[0, me], up_all.at[0, me], up_ssem.at[0, k], up_rsem.at[0, me], layer, others[k]
        )

    def next_up():
        return remote(up_all.at[0, me], up_next, next_ssem, next_rsem, layer - 1, me)

    def first_down():
        return remote(own_down, down_first, first_ssem, first_rsem, layer - 1, me)

    def up_step(t, k):
        return remote(
            up_send.at[t], up_all.at[t + 1, me], up_ssem.at[t + 1, k], up_rsem.at[t + 1, me],
            layer + 1, others[k],
        )

    def last_up():
        return remote(up_send.at[STEPS - 1], up_last, last_ssem, last_rsem, layer + 1, me)

    def part_step(t, k):
        to_layer = layer if t == STEPS - 1 else layer - 1
        return remote(
            part_send.at[t, k], part.at[t, me], part_ssem.at[t, k], part_rsem.at[t, me],
            to_layer, others[k],
        )

    def arrived(ref, rsem):
        remote(ref, ref, next_ssem, rsem, layer, me).wait_recv()

    for k in range(1, n):
        gather(k).start()

    @pl.when(has_below)
    def _():
        first_down().start()
        next_up().start()

    rank_index = lax.broadcasted_iota(jnp.int32, (sources, max_rank), 1)

    def coefficients(trace, factor, block):
        product = lax.dot_general(
            trace, factor.reshape(2 * max_rank, width), (((1,), (1,)), ((), ())),
            preferred_element_type=jnp.float32,
        )
        keep = rank_index < (max_rank // 4) * rank_ref[0, 0, block]
        real = product[:sources, :max_rank] - product[sources:, max_rank:]
        imag = product[:sources, max_rank:] + product[sources:, :max_rank]
        real = jnp.where(keep, real, 0.0)
        imag = jnp.where(keep, imag, 0.0)
        return jnp.concatenate(
            [jnp.concatenate([real, -imag], axis=1), jnp.concatenate([imag, real], axis=1)], axis=0
        ).astype(jnp.bfloat16)

    def expand(coef, factor):
        return jnp.dot(
            coef, factor.reshape(2 * max_rank, width), preferred_element_type=jnp.float32
        )

    load_v.wait()
    load_u.wait()

    for t in range(STEPS):
        held = 0 if t == 0 else jnp.where(has_below, t, 0)
        if t > 0:

            @pl.when(has_below)
            def _():
                for k in range(n):
                    arrived(up_all.at[t, others[k]], up_rsem.at[t, others[k]])

        else:
            for k in range(1, n):
                arrived(up_all.at[0, others[k]], up_rsem.at[0, others[k]])

            @pl.when(has_above)
            def _():
                arrived(up_next, next_rsem)

        total = up_next[...].astype(jnp.float32)
        for k in range(n):
            block = others[k]
            coef = coefficients(up_all[held, block], v_mem[block], block)
            total = total + expand(coef, u_mem[block])
        up_send[t] = total.astype(jnp.bfloat16)

        @pl.when(has_above)
        def _():
            if t < STEPS - 1:
                for k in range(n):
                    up_step(t, k).start()
            else:
                last_up().start()

        @pl.when(has_above)
        def _():
            if t == 0:
                arrived(down_first, first_rsem)
            else:
                for k in range(n):
                    arrived(part.at[t - 1, others[k]], part_rsem.at[t - 1, others[k]])

        down = down_first[...]
        if t > 0:
            total = down.astype(jnp.float32)
            for k in range(n):
                total = total + part[t - 1, others[k]].astype(jnp.float32)
            down = total.astype(jnp.bfloat16)
        last = t == STEPS - 1
        own_part = None
        for k in [*range(1, n), 0]:
            block = others[k]
            piece = expand(coefficients(down, u_mem[block], block), v_mem[block])
            if last and k == 0:
                own_part = piece
            else:
                part_send[t, k] = piece.astype(jnp.bfloat16)
        if last:
            for k in range(1, n):
                part_step(t, k).start()
        else:

            @pl.when(has_below)
            def _():
                for k in [*range(1, n), 0]:
                    part_step(t, k).start()

    total = own_down[...].astype(jnp.float32) + own_part
    for k in range(1, n):
        arrived(part.at[STEPS - 1, others[k]], part_rsem.at[STEPS - 1, others[k]])
        total = total + part[STEPS - 1, others[k]].astype(jnp.float32)
    down_out[0] = total.astype(jnp.bfloat16).reshape(2, sources, width)

    @pl.when(has_below)
    def _():
        arrived(up_last, last_rsem)
        up_out[0] = up_last[...].reshape(2, sources, width)

    @pl.when(jnp.logical_not(has_below))
    def _():
        up_out[0] = up_all[0, me].reshape(2, sources, width)

    for k in range(1, n):
        gather(k).wait_send()
        part_step(STEPS - 1, k).wait_send()

    @pl.when(has_below)
    def _():
        first_down().wait_send()
        next_up().wait_send()
        for t in range(STEPS - 1):
            for k in range(n):
                part_step(t, k).wait_send()

    @pl.when(has_above)
    def _():
        for t in range(STEPS - 1):
            for k in range(n):
                up_step(t, k).wait_send()
        last_up().wait_send()


def solution(mesh):
    layers, n = mesh.shape["gz"], mesh.shape["xy"]

    def on_device(up_source, down_source, source_layer, u_factor, v_factor, block_rank):
        _, _, sources, width = up_source.shape
        rows = 2 * sources
        trace = (rows, width)
        vmem = pl.BlockSpec(memory_space=pltpu.VMEM)
        smem = pl.BlockSpec(memory_space=pltpu.SMEM)
        anywhere = pl.BlockSpec(memory_space=pl.ANY)
        dma = pltpu.SemaphoreType.DMA
        return pl.pallas_call(
            functools.partial(kernel, layers, n),
            out_shape=(
                jax.ShapeDtypeStruct(up_source.shape, jnp.bfloat16),
                jax.ShapeDtypeStruct(down_source.shape, jnp.bfloat16),
            ),
            in_specs=[vmem, vmem, vmem, anywhere, anywhere, smem],
            out_specs=(vmem, vmem),
            scratch_shapes=[
                pltpu.VMEM(u_factor.shape[2:], jnp.bfloat16),
                pltpu.VMEM(v_factor.shape[2:], jnp.bfloat16),
                pltpu.VMEM((STEPS, n, *trace), jnp.bfloat16),
                pltpu.VMEM((STEPS, *trace), jnp.bfloat16),
                pltpu.VMEM(trace, jnp.bfloat16),
                pltpu.VMEM(trace, jnp.bfloat16),
                pltpu.VMEM(trace, jnp.bfloat16),
                pltpu.VMEM(trace, jnp.bfloat16),
                pltpu.VMEM((STEPS, n, *trace), jnp.bfloat16),
                pltpu.VMEM((STEPS, n, *trace), jnp.bfloat16),
                dma((2,)),
                dma((STEPS, n)),
                dma((STEPS, n)),
                dma,
                dma,
                dma,
                dma,
                dma,
                dma,
                dma((STEPS, n)),
                dma((STEPS, n)),
            ],
            compiler_params=pltpu.CompilerParams(collective_id=0, has_side_effects=True),
        )(up_source, down_source, source_layer.reshape(1, sources), u_factor, v_factor, block_rank)

    in_specs = (
        P("gz", None, None, "xy"),
        P("gz", None, None, "xy"),
        P(),
        P("gz", "xy", None, None, None, None),
        P("gz", "xy", None, None, None, None),
        P("gz", "xy", None),
    )
    out_specs = (P("gz", None, None, "xy"), P("gz", None, None, "xy"))
    return jax.shard_map(
        on_device, mesh=mesh, in_specs=in_specs, out_specs=out_specs, check_vma=False
    )
```

time: 87.8 us -> 32.4 us (0.37)
  starting transfers between devices: 31.9 us -> 0 us
  Pallas kernels: 0 us -> 29.2 us
  blocking collectives: 22.2 us -> 0 us
  waiting for transfers between devices: 18.6 us -> 0 us
  matrix products: 6 us -> 0 us
  other arithmetic: 3 us -> 0 us
  local copies, waits for them, and re-layouts: 4.16 us -> 2 us
    pallas_call x0 -> x1, Pallas kernels: none -> 29.2 us  [on_device(): pl.pallas_call(functools.partial(kernel, layers, n), out_shape=(jax.Shape...]
    all_gather x3 -> x0, blocking collectives: 22.2 us -> none  [advance(): gathered = lax.all_gather(up_part, 'xy', axis=2, tiled=True)]
    ppermute x6 -> x0, starting transfers between devices: 18.5 us -> none  [from_behind(): return lax.ppermute(block, axis, route)]
    all_to_all x4 -> x0, starting transfers between devices: 13.3 us -> none  [the longest x3 9.85 us: advance(): lax.all_to_all(down_coef, 'xy', split_axis=1, concat_axis=0, tiled=True)]
    all_to_all x4 -> x0, waiting for transfers between devices: 11.4 us -> none  [the longest x3 11.4 us: advance(): lax.all_to_all(down_coef, 'xy', split_axis=1, concat_axis=0, tiled=True)]
    ppermute x6 -> x0, waiting for transfers between devices: 7.18 us -> none  [from_behind(): return lax.ppermute(block, axis, route)]
    dot_general x12 -> x0, matrix products: 6 us -> none  [the longest x3 3.95 us: advance(): jnp.einsum('asjb,ijcrb->ijascr', pieces, v_layer, preferred_element_type=...]
    convert_element_type x3 -> x0, local copies, waits for them, and re-layouts: 1.86 us -> none  [advance(): jnp.where(keep_rank[:, :, None, None, :], down_coef, 0.0)]
  transfers between devices with their start and end apart: 10 -> 0, of which waited for: 5 -> 0; matrix products, arithmetic and copies ran while one was open for 7% -> 0% of each run, Pallas kernels for 0% -> 0%
where the time goes in v1:
time: 32.4 us; the launch traced here: 31.9 us
  Pallas kernels  29.2 us (90%)
  local copies, waits for them, and re-layouts  2 us (6%)
  between operations  0.65 us (2%)
    pallas_call x1, Pallas kernels, on_device(): pl.pallas_call(functools.partial(kernel, layers, n), out_shape=(jax.Shape...  29.2 us
    unnamed x4, local copies, waits for them, and re-layouts  2 us

profile of v1, /device:TPU:0, one launch (start us, length us, event | category | flops | bytes accessed | tf_op | source)
XLA Modules:
  0.0 31.9 jit_solution(16718930282549472277)
XLA Ops:
  0.6 29.2 %shard_map.77 = (bf16[1,2,32,256]{3,2,1,0:T(8,128)(2,1)}, bf16[1,2,32,256]{3,2,1,0:T(8,128)(2,1)}) custom-call(bf16[1,2,32,256]{3,2,1,0:T(8,128)(2,1)} %up_ref.1, bf16[1,2,32,256]{3,2,1,0:T(8,128)(2,1)} %down_ref.1, s32[1,32]{1,0:T(1,128)} %bitcast.1, bf16[1,1,4,2,128,256]{5,4,3,2,1,0:T(8,128)(2,1)} %u_hbm.1, bf16[1,1,4,2,128,256]{5,4,3,2,1,0:T(8,128)(2,1)} %v_hbm.1, ...), custom_call_target="tpu_custom_call" | custom-call | tf_op jit(solution)/shard_map/pallas_call | solution.py:258
  29.8 0.0 copy-start
  29.9 1.4 %copy.10 = bf16[1,2,32,256]{3,2,1,0:T(8,128)(2,1)} copy(bf16[1,2,32,256]{3,2,1,0:T(8,128)(2,1)} %get-tuple-element.4) | data formatting | bytes 65536
  31.2 0.0 copy-done
  31.2 0.6 %copy.11 = bf16[1,2,32,256]{3,2,1,0:T(8,128)(2,1)} copy(bf16[1,2,32,256]{3,2,1,0:T(8,128)(2,1)S(1)} %copy-done) | data formatting | bytes 65536
Async XLA Ops:
  29.8 1.4 %copy-start = (bf16[1,2,32,256]{3,2,1,0:T(8,128)(2,1)S(1)}, bf16[1,2,32,256]{3,2,1,0:T(8,128)(2,1)}, u32[]{:S(2)}) copy-start(bf16[1,2,32,256]{3,2,1,0:T(8,128)(2,1)} %get-tuple-element.5) | copy-start | bytes 98308

commit v2 on v1

--- a/solution.py
+++ b/solution.py
@@ -14,8 +14,10 @@
 def kernel(
     layers, n, up_ref, down_ref, layer_ref, u_hbm, v_hbm, rank_ref, up_out, down_out,
     u_mem, v_mem, up_all, up_send, up_next, up_last, own_down, down_first, part, part_send,
+    twin_part, twin_send, last_in, last_send,
     load_sem, up_ssem, up_rsem, next_ssem, next_rsem, last_ssem, last_rsem,
     first_ssem, first_rsem, part_ssem, part_rsem,
+    relay_ssem, twin_ssem, twin_rsem, last_part_ssem, last_part_rsem,
 ):
     layer = lax.axis_index("gz")
     me = lax.axis_index("xy")
@@ -25,6 +27,11 @@
     sources = rows // 2
     max_rank = u_mem.shape[2]
     others = [lax.rem(me + k, n) for k in range(n)]
+    core = lax.rem(me, 2)
+    twin = me + 1 - 2 * core
+    like = [lax.rem(me + 2 * k, n) for k in range(n // 2)]
+    unlike = [lax.rem(twin + 2 * k, n) for k in range(n // 2)]
+    chip = me // 2
 
     def remote(src, dst, ssem, rsem, to_layer, to_block):
         return pltpu.make_async_remote_copy(
@@ -49,13 +56,13 @@
 
     @pl.when(has_above)
     def _():
-        for k in range(n):
-            greet(layer + 1, others[k])
+        for k in range(n // 2):
+            greet(layer + 1, like[k])
 
     @pl.when(has_below)
     def _():
-        for k in range(n):
-            greet(layer - 1, others[k])
+        for k in range(n // 2):
+            greet(layer - 1, like[k])
 
     square = (sources, sources)
     diagonal = lax.broadcasted_iota(jnp.int32, square, 0) == lax.broadcasted_iota(jnp.int32, square, 1)
@@ -79,7 +86,7 @@
         part[0] = jnp.zeros_like(part[0])
         part[1] = jnp.zeros_like(part[1])
 
-    peers = n - 1 + jnp.where(has_above, n, 0) + jnp.where(has_below, n, 0)
+    peers = n - 1 + jnp.where(has_above, n // 2, 0) + jnp.where(has_below, n // 2, 0)
     pl.semaphore_wait(barrier, peers)
 
     def gather(k):
@@ -96,17 +103,33 @@
     def up_step(t, k):
         return remote(
             up_send.at[t], up_all.at[t + 1, me], up_ssem.at[t + 1, k], up_rsem.at[t + 1, me],
-            layer + 1, others[k],
-        )
+            layer + 1, like[k],
+        )
+
+    def relay(t, k):
+        slot = up_all.at[t, like[k]]
+        return remote(slot, slot, relay_ssem.at[t - 1, k], up_rsem.at[t, like[k]], layer, twin)
 
     def last_up():
         return remote(up_send.at[STEPS - 1], up_last, last_ssem, last_rsem, layer + 1, me)
 
     def part_step(t, k):
-        to_layer = layer if t == STEPS - 1 else layer - 1
-        return remote(
-            part_send.at[t, k], part.at[t, me], part_ssem.at[t, k], part_rsem.at[t, me],
-            to_layer, others[k],
+        return remote(
+            part_send.at[t, k], part.at[t, chip], part_ssem.at[t, k], part_rsem.at[t, chip],
+            layer - 1, like[k],
+        )
+
+    def twin_step(t, k):
+        place = unlike[k] // 2
+        return remote(
+            twin_send.at[t, k], twin_part.at[t, place], twin_ssem.at[t, k], twin_rsem.at[t, place],
+            layer, twin,
+        )
+
+    def last_part(k):
+        return remote(
+            last_send.at[k], last_in.at[me], last_part_ssem.at[k], last_part_rsem.at[me],
+            layer, others[k],
         )
 
     def arrived(ref, rsem):
@@ -150,8 +173,11 @@
 
             @pl.when(has_below)
             def _():
-                for k in range(n):
-                    arrived(up_all.at[t, others[k]], up_rsem.at[t, others[k]])
+                for k in range(n // 2):
+                    arrived(up_all.at[t, like[k]], up_rsem.at[t, like[k]])
+                    relay(t, k).start()
+                for k in range(n // 2):
+                    arrived(up_all.at[t, unlike[k]], up_rsem.at[t, unlike[k]])
 
         else:
             for k in range(1, n):
@@ -171,7 +197,7 @@
         @pl.when(has_above)
         def _():
             if t < STEPS - 1:
-                for k in range(n):
+                for k in reversed(range(n // 2)):
                     up_step(t, k).start()
             else:
                 last_up().start()
@@ -181,38 +207,47 @@
             if t == 0:
                 arrived(down_first, first_rsem)
             else:
-                for k in range(n):
-                    arrived(part.at[t - 1, others[k]], part_rsem.at[t - 1, others[k]])
+                for k in range(n // 2):
+                    place = like[k] // 2
+                    arrived(part.at[t - 1, place], part_rsem.at[t - 1, place])
 
         down = down_first[...]
         if t > 0:
             total = down.astype(jnp.float32)
-            for k in range(n):
-                total = total + part[t - 1, others[k]].astype(jnp.float32)
+            for k in range(n // 2):
+                total = total + part[t - 1, like[k] // 2].astype(jnp.float32)
             down = total.astype(jnp.bfloat16)
-        last = t == STEPS - 1
-        own_part = None
-        for k in [*range(1, n), 0]:
-            block = others[k]
-            piece = expand(coefficients(down, u_mem[block], block), v_mem[block])
-            if last and k == 0:
-                own_part = piece
-            else:
-                part_send[t, k] = piece.astype(jnp.bfloat16)
-        if last:
-            for k in range(1, n):
-                part_step(t, k).start()
-        else:
+
+        def piece(block):
+            return expand(coefficients(down, u_mem[block], block), v_mem[block])
+
+        if t < STEPS - 1:
+            for k in range(n // 2):
+                twin_send[t, k] = piece(unlike[k]).astype(jnp.bfloat16)
+                twin_step(t, k).start()
+            pieces = [piece(like[k]) for k in range(n // 2)]
+            for k in range(n // 2):
+                place = like[k] // 2
+                arrived(twin_part.at[t, place], twin_rsem.at[t, place])
+                part_send[t, k] = (pieces[k] + twin_part[t, place].astype(jnp.float32)).astype(
+                    jnp.bfloat16
+                )
 
             @pl.when(has_below)
             def _():
-                for k in [*range(1, n), 0]:
+                for k in reversed(range(n // 2)):
                     part_step(t, k).start()
+
+        else:
+            for k in range(1, n):
+                last_send[k] = piece(others[k]).astype(jnp.bfloat16)
+                last_part(k).start()
+            own_part = piece(me)
 
     total = own_down[...].astype(jnp.float32) + own_part
     for k in range(1, n):
-        arrived(part.at[STEPS - 1, others[k]], part_rsem.at[STEPS - 1, others[k]])
-        total = total + part[STEPS - 1, others[k]].astype(jnp.float32)
+        arrived(last_in.at[others[k]], last_part_rsem.at[others[k]])
+        total = total + last_in[others[k]].astype(jnp.float32)
     down_out[0] = total.astype(jnp.bfloat16).reshape(2, sources, width)
 
     @pl.when(has_below)
@@ -226,20 +261,24 @@
 
     for k in range(1, n):
         gather(k).wait_send()
-        part_step(STEPS - 1, k).wait_send()
+        last_part(k).wait_send()
+    for t in range(STEPS - 1):
+        for k in range(n // 2):
+            twin_step(t, k).wait_send()
 
     @pl.when(has_below)
     def _():
         first_down().wait_send()
         next_up().wait_send()
         for t in range(STEPS - 1):
-            for k in range(n):
+            for k in range(n // 2):
                 part_step(t, k).wait_send()
+                relay(t + 1, k).wait_send()
 
     @pl.when(has_above)
     def _():
         for t in range(STEPS - 1):
-            for k in range(n):
+            for k in range(n // 2):
                 up_step(t, k).wait_send()
         last_up().wait_send()
 
@@ -272,8 +311,12 @@
                 pltpu.VMEM(trace, jnp.bfloat16),
                 pltpu.VMEM(trace, jnp.bfloat16),
                 pltpu.VMEM(trace, jnp.bfloat16),
-                pltpu.VMEM((STEPS, n, *trace), jnp.bfloat16),
-                pltpu.VMEM((STEPS, n, *trace), jnp.bfloat16),
+                pltpu.VMEM((STEPS - 1, n // 2, *trace), jnp.bfloat16),
+                pltpu.VMEM((STEPS - 1, n // 2, *trace), jnp.bfloat16),
+                pltpu.VMEM((STEPS - 1, n // 2, *trace), jnp.bfloat16),
+                pltpu.VMEM((STEPS - 1, n // 2, *trace), jnp.bfloat16),
+                pltpu.VMEM((n, *trace), jnp.bfloat16),
+                pltpu.VMEM((n, *trace), jnp.bfloat16),
                 dma((2,)),
                 dma((STEPS, n)),
                 dma((STEPS, n)),
@@ -283,8 +326,13 @@
                 dma,
                 dma,
                 dma,
-                dma((STEPS, n)),
-                dma((STEPS, n)),
+                dma((STEPS - 1, n // 2)),
+                dma((STEPS - 1, n // 2)),
+                dma((STEPS - 1, n // 2)),
+                dma((STEPS - 1, n // 2)),
+                dma((STEPS - 1, n // 2)),
+                dma((n,)),
+                dma((n,)),
             ],
             compiler_params=pltpu.CompilerParams(collective_id=0, has_side_effects=True),
         )(up_source, down_source, source_layer.reshape(1, sources), u_factor, v_factor, block_rank)

time: 32.4 us -> 28.7 us (0.89)
  Pallas kernels: 29.2 us -> 25.8 us
    pallas_call x1, Pallas kernels: 29.2 us -> 25.8 us  [on_device(): pl.pallas_call(functools.partial(kernel, layers, n), out_shape=(jax.Shape...]
where the time goes in v2:
time: 28.7 us; the launch traced here: 28.4 us
  Pallas kernels  25.8 us (90%)
  local copies, waits for them, and re-layouts  2 us (7%)
  between operations  0.65 us (2%)
    pallas_call x1, Pallas kernels, on_device(): pl.pallas_call(functools.partial(kernel, layers, n), out_shape=(jax.Shape...  25.8 us
    unnamed x4, local copies, waits for them, and re-layouts  2 us

profile of v2, /device:TPU:0, one launch (start us, length us, event | category | flops | bytes accessed | tf_op | source)
XLA Modules:
  0.0 28.4 jit_solution(1934796610671159267)
XLA Ops:
  0.6 25.8 %shard_map.77 = (bf16[1,2,32,256]{3,2,1,0:T(8,128)(2,1)}, bf16[1,2,32,256]{3,2,1,0:T(8,128)(2,1)}) custom-call(bf16[1,2,32,256]{3,2,1,0:T(8,128)(2,1)} %up_ref.1, bf16[1,2,32,256]{3,2,1,0:T(8,128)(2,1)} %down_ref.1, s32[1,32]{1,0:T(1,128)} %bitcast.1, bf16[1,1,4,2,128,256]{5,4,3,2,1,0:T(8,128)(2,1)} %u_hbm.1, bf16[1,1,4,2,128,256]{5,4,3,2,1,0:T(8,128)(2,1)} %v_hbm.1, ...), custom_call_target="tpu_custom_call" | custom-call | tf_op jit(solution)/shard_map/pallas_call | solution.py:297
  26.4 0.0 copy-start
  26.4 1.4 %copy.10 = bf16[1,2,32,256]{3,2,1,0:T(8,128)(2,1)} copy(bf16[1,2,32,256]{3,2,1,0:T(8,128)(2,1)} %get-tuple-element.4) | data formatting | bytes 65536
  27.8 0.0 copy-done
  27.8 0.6 %copy.11 = bf16[1,2,32,256]{3,2,1,0:T(8,128)(2,1)} copy(bf16[1,2,32,256]{3,2,1,0:T(8,128)(2,1)S(1)} %copy-done) | data formatting | bytes 65536
Async XLA Ops:
  26.4 1.4 %copy-start = (bf16[1,2,32,256]{3,2,1,0:T(8,128)(2,1)S(1)}, bf16[1,2,32,256]{3,2,1,0:T(8,128)(2,1)}, u32[]{:S(2)}) copy-start(bf16[1,2,32,256]{3,2,1,0:T(8,128)(2,1)} %get-tuple-element.5) | copy-start | bytes 98308

commit v3 on v2

--- a/solution.py
+++ b/solution.py
@@ -12,7 +12,8 @@
 
 
 def kernel(
-    layers, n, up_ref, down_ref, layer_ref, u_hbm, v_hbm, rank_ref, up_out, down_out,
+    layers, n, up_hbm, down_hbm, layer_hbm, u_hbm, v_hbm, rank_hbm, up_out, down_out,
+    up_ref, down_ref, layer_ref, rank_ref, down_done,
     u_mem, v_mem, up_all, up_send, up_next, up_last, own_down, down_first, part, part_send,
     twin_part, twin_send, last_in, last_send,
     load_sem, up_ssem, up_rsem, next_ssem, next_rsem, last_ssem, last_rsem,
@@ -41,8 +42,14 @@
 
     load_u = pltpu.make_async_copy(u_hbm.at[0, 0], u_mem, load_sem.at[0])
     load_v = pltpu.make_async_copy(v_hbm.at[0, 0], v_mem, load_sem.at[1])
-    load_v.start()
-    load_u.start()
+    small = [
+        pltpu.make_async_copy(src, dst, load_sem.at[2 + i])
+        for i, (src, dst) in enumerate(
+            [(layer_hbm, layer_ref), (up_hbm.at[0], up_ref), (down_hbm.at[0], down_ref), (rank_hbm, rank_ref)]
+        )
+    ]
+    for load in small:
+        load.start()
 
     barrier = pltpu.get_barrier_semaphore()
 
@@ -64,6 +71,10 @@
         for k in range(n // 2):
             greet(layer - 1, like[k])
 
+    load_v.start()
+    load_u.start()
+    for load in small:
+        load.wait()
     square = (sources, sources)
     diagonal = lax.broadcasted_iota(jnp.int32, square, 0) == lax.broadcasted_iota(jnp.int32, square, 1)
     source_layer = jnp.sum(
@@ -71,10 +82,10 @@
     )
     source_layer = jnp.broadcast_to(jnp.concatenate([source_layer, source_layer], axis=0), (rows, width))
     up_own = jnp.where(
-        layer >= source_layer, up_ref[0].reshape(rows, width).astype(jnp.float32), 0.0
+        layer >= source_layer, up_ref[...].reshape(rows, width).astype(jnp.float32), 0.0
     ).astype(jnp.bfloat16)
     down_own = jnp.where(
-        layer <= source_layer, down_ref[0].reshape(rows, width).astype(jnp.float32), 0.0
+        layer <= source_layer, down_ref[...].reshape(rows, width).astype(jnp.float32), 0.0
     ).astype(jnp.bfloat16)
     up_all[0, me] = up_own
     own_down[...] = down_own
@@ -248,16 +259,21 @@
     for k in range(1, n):
         arrived(last_in.at[others[k]], last_part_rsem.at[others[k]])
         total = total + last_in[others[k]].astype(jnp.float32)
-    down_out[0] = total.astype(jnp.bfloat16).reshape(2, sources, width)
+    down_done[...] = total.astype(jnp.bfloat16).reshape(2, sources, width)
+    put_down = pltpu.make_async_copy(down_done, down_out.at[0], load_sem.at[0])
+    put_down.start()
 
     @pl.when(has_below)
     def _():
         arrived(up_last, last_rsem)
-        up_out[0] = up_last[...].reshape(2, sources, width)
+        up_ref[...] = up_last[...].reshape(2, sources, width)
 
     @pl.when(jnp.logical_not(has_below))
     def _():
-        up_out[0] = up_all[0, me].reshape(2, sources, width)
+        up_ref[...] = up_all[0, me].reshape(2, sources, width)
+
+    put_up = pltpu.make_async_copy(up_ref, up_out.at[0], load_sem.at[1])
+    put_up.start()
 
     for k in range(1, n):
         gather(k).wait_send()
@@ -282,6 +298,9 @@
                 up_step(t, k).wait_send()
         last_up().wait_send()
 
+    put_down.wait()
+    put_up.wait()
+
 
 def solution(mesh):
     layers, n = mesh.shape["gz"], mesh.shape["xy"]
@@ -290,9 +309,9 @@
         _, _, sources, width = up_source.shape
         rows = 2 * sources
         trace = (rows, width)
-        vmem = pl.BlockSpec(memory_space=pltpu.VMEM)
-        smem = pl.BlockSpec(memory_space=pltpu.SMEM)
         anywhere = pl.BlockSpec(memory_space=pl.ANY)
+        hbm = pl.BlockSpec(memory_space=pltpu.HBM)
+        grant = (4 << 20) + 8 * u_factor.size
         dma = pltpu.SemaphoreType.DMA
         return pl.pallas_call(
             functools.partial(kernel, layers, n),
@@ -300,9 +319,14 @@
                 jax.ShapeDtypeStruct(up_source.shape, jnp.bfloat16),
                 jax.ShapeDtypeStruct(down_source.shape, jnp.bfloat16),
             ),
-            in_specs=[vmem, vmem, vmem, anywhere, anywhere, smem],
-            out_specs=(vmem, vmem),
+            in_specs=[hbm] * 6,
+            out_specs=(anywhere, anywhere),
             scratch_shapes=[
+                pltpu.VMEM((2, sources, width), jnp.bfloat16),
+                pltpu.VMEM((2, sources, width), jnp.bfloat16),
+                pltpu.VMEM((1, sources), jnp.int32),
+                pltpu.SMEM(block_rank.shape, jnp.int32),
+                pltpu.VMEM((2, sources, width), jnp.bfloat16),
                 pltpu.VMEM(u_factor.shape[2:], jnp.bfloat16),
                 pltpu.VMEM(v_factor.shape[2:], jnp.bfloat16),
                 pltpu.VMEM((STEPS, n, *trace), jnp.bfloat16),
@@ -317,7 +341,7 @@
                 pltpu.VMEM((STEPS - 1, n // 2, *trace), jnp.bfloat16),
                 pltpu.VMEM((n, *trace), jnp.bfloat16),
                 pltpu.VMEM((n, *trace), jnp.bfloat16),
-                dma((2,)),
+                dma((6,)),
                 dma((STEPS, n)),
                 dma((STEPS, n)),
                 dma,
@@ -334,7 +358,9 @@
                 dma((n,)),
                 dma((n,)),
             ],
-            compiler_params=pltpu.CompilerParams(collective_id=0, has_side_effects=True),
+            compiler_params=pltpu.CompilerParams(
+                collective_id=0, has_side_effects=True, vmem_limit_bytes=grant
+            ),
         )(up_source, down_source, source_layer.reshape(1, sources), u_factor, v_factor, block_rank)
 
     in_specs = (

time: 28.7 us -> 31 us (1.080)
  local copies, waits for them, and re-layouts: 2 us -> 5.48 us
  Pallas kernels: 25.8 us -> 24.5 us
    unnamed x4 -> x14, local copies, waits for them, and re-layouts: 2 us -> 5.48 us
    pallas_call x1, Pallas kernels: 25.8 us -> 24.5 us  [on_device(): pl.pallas_call(functools.partial(kernel, layers, n), out_shape=(jax.Shape...]
where the time goes in v3:
time: 31 us; the launch traced here: 30.7 us
  Pallas kernels  24.5 us (79%)
  local copies, waits for them, and re-layouts  5.48 us (18%)
  between operations  0.66 us (2%)
    pallas_call x1, Pallas kernels, on_device(): pl.pallas_call(functools.partial(kernel, layers, n), out_shape=(jax.Shape...  24.5 us
    unnamed x14, local copies, waits for them, and re-layouts  5.48 us

profile of v3, /device:TPU:0, one launch (start us, length us, event | category | flops | bytes accessed | tf_op | source)
XLA Modules:
  0.0 30.7 jit_solution(14047502527190796771)
XLA Ops:
  0.6 0.0 copy-start.5
  0.6 0.0 copy-start.4
  0.7 0.6 %copy-done.5 = s32[1,1,4]{2,1,0:T(1,128)S(1)} copy-done((s32[1,1,4]{2,1,0:T(1,128)S(1)}, s32[1,1,4]{2,1,0:T(1,128)}, u32[]{:S(2)}) %copy-start.5) | copy-done | bytes 40
  1.3 0.0 copy-done.4
  1.3 0.0 copy-start
  1.3 1.0 %copy-done = bf16[1,1,4,2,128,256]{5,4,3,2,1,0:T(8,128)(2,1)S(1)} copy-done((bf16[1,1,4,2,128,256]{5,4,3,2,1,0:T(8,128)(2,1)S(1)}, bf16[1,1,4,2,128,256]{5,4,3,2,1,0:T(8,128)(2,1)}, u32[]{:S(2)}) %copy-start) | copy-done | bytes 524312
  2.3 0.0 copy-start.1
  2.3 1.0 %copy-done.1 = bf16[1,1,4,2,128,256]{5,4,3,2,1,0:T(8,128)(2,1)S(1)} copy-done((bf16[1,1,4,2,128,256]{5,4,3,2,1,0:T(8,128)(2,1)S(1)}, bf16[1,1,4,2,128,256]{5,4,3,2,1,0:T(8,128)(2,1)}, u32[]{:S(2)}) %copy-start.1) | copy-done | bytes 524312
  3.4 0.0 copy-start.2
  3.4 0.8 %copy-done.2 = bf16[1,2,32,256]{3,2,1,0:T(8,128)(2,1)S(1)} copy-done((bf16[1,2,32,256]{3,2,1,0:T(8,128)(2,1)S(1)}, bf16[1,2,32,256]{3,2,1,0:T(8,128)(2,1)}, u32[]{:S(2)}) %copy-start.2) | copy-done | bytes 32792
  4.1 0.0 copy-start.3
  4.1 0.8 %copy-done.3 = bf16[1,2,32,256]{3,2,1,0:T(8,128)(2,1)S(1)} copy-done((bf16[1,2,32,256]{3,2,1,0:T(8,128)(2,1)S(1)}, bf16[1,2,32,256]{3,2,1,0:T(8,128)(2,1)}, u32[]{:S(2)}) %copy-start.3) | copy-done | bytes 32792
  4.9 24.5 %shard_map.77 = (bf16[1,2,32,256]{3,2,1,0:T(8,128)(2,1)S(1)}, bf16[1,2,32,256]{3,2,1,0:T(8,128)(2,1)S(1)}) custom-call(bf16[1,2,32,256]{3,2,1,0:T(8,128)(2,1)S(1)} %copy-done.2, bf16[1,2,32,256]{3,2,1,0:T(8,128)(2,1)S(1)} %copy-done.3, s32[1,32]{1,0:T(1,128)S(1)} %bitcast.1, bf16[1,1,4,2,128,256]{5,4,3,2,1,0:T(8,128)(2,1)S(1)} %copy-done, ...), custom_call_target="tpu_custom_call" | custom-call | tf_op jit(solution)/shard_map/pallas_call | solution.py:316
  29.4 0.6 %copy.10 = bf16[1,2,32,256]{3,2,1,0:T(8,128)(2,1)} copy(bf16[1,2,32,256]{3,2,1,0:T(8,128)(2,1)S(1)} %get-tuple-element.4) | data formatting | bytes 65536
  30.1 0.6 %copy.11 = bf16[1,2,32,256]{3,2,1,0:T(8,128)(2,1)} copy(bf16[1,2,32,256]{3,2,1,0:T(8,128)(2,1)S(1)} %get-tuple-element.5) | data formatting | bytes 65536
Async XLA Ops:
  0.6 0.7 %copy-start.5 = (s32[1,1,4]{2,1,0:T(1,128)S(1)}, s32[1,1,4]{2,1,0:T(1,128)}, u32[]{:S(2)}) copy-start(s32[1,1,4]{2,1,0:T(1,128)} %rank_hbm.1) | copy-start | bytes 52
  0.6 0.7 %copy-start.4 = (s32[32]{0:T(128)S(1)}, s32[32]{0:T(128)}, u32[]{:S(2)}) copy-start(s32[32]{0:T(128)} %param.8) | copy-start | bytes 388
  1.3 1.0 %copy-start = (bf16[1,1,4,2,128,256]{5,4,3,2,1,0:T(8,128)(2,1)S(1)}, bf16[1,1,4,2,128,256]{5,4,3,2,1,0:T(8,128)(2,1)}, u32[]{:S(2)}) copy-start(bf16[1,1,4,2,128,256]{5,4,3,2,1,0:T(8,128)(2,1)} %u_hbm.1) | copy-start | bytes 1572868
  2.3 1.0 %copy-start.1 = (bf16[1,1,4,2,128,256]{5,4,3,2,1,0:T(8,128)(2,1)S(1)}, bf16[1,1,4,2,128,256]{5,4,3,2,1,0:T(8,128)(2,1)}, u32[]{:S(2)}) copy-start(bf16[1,1,4,2,128,256]{5,4,3,2,1,0:T(8,128)(2,1)} %v_hbm.1) | copy-start | bytes 1572868
  3.4 0.8 %copy-start.2 = (bf16[1,2,32,256]{3,2,1,0:T(8,128)(2,1)S(1)}, bf16[1,2,32,256]{3,2,1,0:T(8,128)(2,1)}, u32[]{:S(2)}) copy-start(bf16[1,2,32,256]{3,2,1,0:T(8,128)(2,1)} %up_hbm.1) | copy-start | bytes 98308
  4.1 0.8 %copy-start.3 = (bf16[1,2,32,256]{3,2,1,0:T(8,128)(2,1)S(1)}, bf16[1,2,32,256]{3,2,1,0:T(8,128)(2,1)}, u32[]{:S(2)}) copy-start(bf16[1,2,32,256]{3,2,1,0:T(8,128)(2,1)} %down_hbm.1) | copy-start | bytes 98308

commit v4 on v3

--- a/solution.py
+++ b/solution.py
@@ -311,7 +311,6 @@
         trace = (rows, width)
         anywhere = pl.BlockSpec(memory_space=pl.ANY)
         hbm = pl.BlockSpec(memory_space=pltpu.HBM)
-        grant = (4 << 20) + 8 * u_factor.size
         dma = pltpu.SemaphoreType.DMA
         return pl.pallas_call(
             functools.partial(kernel, layers, n),
@@ -359,7 +358,7 @@
                 dma((n,)),
             ],
             compiler_params=pltpu.CompilerParams(
-                collective_id=0, has_side_effects=True, vmem_limit_bytes=grant
+                collective_id=0, has_side_effects=True
             ),
         )(up_source, down_source, source_layer.reshape(1, sources), u_factor, v_factor, block_rank)
 

time: 31 us -> 27.8 us (0.90)
  local copies, waits for them, and re-layouts: 5.48 us -> 2 us
  Pallas kernels: 24.5 us -> 25 us
    unnamed x14 -> x4, local copies, waits for them, and re-layouts: 5.48 us -> 2 us
    pallas_call x1, Pallas kernels: 24.5 us -> 25 us  [on_device(): pl.pallas_call(functools.partial(kernel, layers, n), out_shape=(jax.Shape...]
where the time goes in v4:
time: 27.8 us; the launch traced here: 27.6 us
  Pallas kernels  25 us (90%)
  local copies, waits for them, and re-layouts  2 us (7%)
  between operations  0.65 us (2%)
    pallas_call x1, Pallas kernels, on_device(): pl.pallas_call(functools.partial(kernel, layers, n), out_shape=(jax.Shape...  25 us
    unnamed x4, local copies, waits for them, and re-layouts  2 us

profile of v4, /device:TPU:0, one launch (start us, length us, event | category | flops | bytes accessed | tf_op | source)
XLA Modules:
  0.0 27.6 jit_solution(13522349968616730694)
XLA Ops:
  0.6 25.0 %shard_map.77 = (bf16[1,2,32,256]{3,2,1,0:T(8,128)(2,1)}, bf16[1,2,32,256]{3,2,1,0:T(8,128)(2,1)}) custom-call(bf16[1,2,32,256]{3,2,1,0:T(8,128)(2,1)} %up_hbm.1, bf16[1,2,32,256]{3,2,1,0:T(8,128)(2,1)} %down_hbm.1, s32[1,32]{1,0:T(1,128)} %bitcast.1, bf16[1,1,4,2,128,256]{5,4,3,2,1,0:T(8,128)(2,1)} %u_hbm.1, bf16[1,1,4,2,128,256]{5,4,3,2,1,0:T(8,128)(2,1)} %v_hbm.1, ...), custom_call_target="tpu_custom_call" | custom-call | tf_op jit(solution)/shard_map/pallas_call | solution.py:315
  25.6 0.0 copy-start
  25.6 1.4 %copy.10 = bf16[1,2,32,256]{3,2,1,0:T(8,128)(2,1)} copy(bf16[1,2,32,256]{3,2,1,0:T(8,128)(2,1)} %get-tuple-element.4) | data formatting | bytes 65536
  27.0 0.0 copy-done
  27.0 0.6 %copy.11 = bf16[1,2,32,256]{3,2,1,0:T(8,128)(2,1)} copy(bf16[1,2,32,256]{3,2,1,0:T(8,128)(2,1)S(1)} %copy-done) | data formatting | bytes 65536
Async XLA Ops:
  25.6 1.4 %copy-start = (bf16[1,2,32,256]{3,2,1,0:T(8,128)(2,1)S(1)}, bf16[1,2,32,256]{3,2,1,0:T(8,128)(2,1)}, u32[]{:S(2)}) copy-start(bf16[1,2,32,256]{3,2,1,0:T(8,128)(2,1)} %get-tuple-element.5) | copy-start | bytes 98308

commit v5 on v4

--- a/solution.py
+++ b/solution.py
@@ -178,40 +178,27 @@
     load_v.wait()
     load_u.wait()
 
+    def wait_blocks(t, blocks):
+        for block in blocks:
+            arrived(up_all.at[t, block], up_rsem.at[t, block])
+
     for t in range(STEPS):
+        last = t == STEPS - 1
         held = 0 if t == 0 else jnp.where(has_below, t, 0)
+
+        def rise(block):
+            return expand(coefficients(up_all[held, block], v_mem[block], block), u_mem[block])
+
+        def piece(block):
+            return expand(coefficients(down, u_mem[block], block), v_mem[block])
+
         if t > 0:
 
             @pl.when(has_below)
             def _():
                 for k in range(n // 2):
-                    arrived(up_all.at[t, like[k]], up_rsem.at[t, like[k]])
+                    wait_blocks(t, [like[k]])
                     relay(t, k).start()
-                for k in range(n // 2):
-                    arrived(up_all.at[t, unlike[k]], up_rsem.at[t, unlike[k]])
-
-        else:
-            for k in range(1, n):
-                arrived(up_all.at[0, others[k]], up_rsem.at[0, others[k]])
-
-            @pl.when(has_above)
-            def _():
-                arrived(up_next, next_rsem)
-
-        total = up_next[...].astype(jnp.float32)
-        for k in range(n):
-            block = others[k]
-            coef = coefficients(up_all[held, block], v_mem[block], block)
-            total = total + expand(coef, u_mem[block])
-        up_send[t] = total.astype(jnp.bfloat16)
-
-        @pl.when(has_above)
-        def _():
-            if t < STEPS - 1:
-                for k in reversed(range(n // 2)):
-                    up_step(t, k).start()
-            else:
-                last_up().start()
 
         @pl.when(has_above)
         def _():
@@ -229,14 +216,46 @@
                 total = total + part[t - 1, like[k] // 2].astype(jnp.float32)
             down = total.astype(jnp.bfloat16)
 
-        def piece(block):
-            return expand(coefficients(down, u_mem[block], block), v_mem[block])
-
-        if t < STEPS - 1:
+        if last:
+            for k in range(1, n):
+                last_send[k] = piece(others[k]).astype(jnp.bfloat16)
+                last_part(k).start()
+        else:
             for k in range(n // 2):
                 twin_send[t, k] = piece(unlike[k]).astype(jnp.bfloat16)
                 twin_step(t, k).start()
-            pieces = [piece(like[k]) for k in range(n // 2)]
+
+        if t == 0:
+            wait_blocks(0, like[1:])
+        total = sum([rise(block) for block in like])
+        if t == 0:
+            wait_blocks(0, unlike)
+
+            @pl.when(has_above)
+            def _():
+                arrived(up_next, next_rsem)
+
+        else:
+
+            @pl.when(has_below)
+            def _():
+                wait_blocks(t, unlike)
+
+        total = total + sum([rise(block) for block in unlike])
+        up_send[t] = (up_next[...].astype(jnp.float32) + total).astype(jnp.bfloat16)
+
+        @pl.when(has_above)
+        def _():
+            if last:
+                last_up().start()
+            else:
+                for k in reversed(range(n // 2)):
+                    up_step(t, k).start()
+
+        if last:
+            own_part = piece(me)
+        else:
+            pieces = [piece(block) for block in like]
             for k in range(n // 2):
                 place = like[k] // 2
                 arrived(twin_part.at[t, place], twin_rsem.at[t, place])
@@ -248,12 +267,6 @@
             def _():
                 for k in reversed(range(n // 2)):
                     part_step(t, k).start()
-
-        else:
-            for k in range(1, n):
-                last_send[k] = piece(others[k]).astype(jnp.bfloat16)
-                last_part(k).start()
-            own_part = piece(me)
 
     total = own_down[...].astype(jnp.float32) + own_part
     for k in range(1, n):

time: 27.8 us -> 27.1 us (0.975)
  the two profiles are of different devices: /device:TPU:0 before, /device:TPU:8 now
where the time goes in v5:
time: 27.1 us; the launch traced here: 26.9 us
  Pallas kernels  24.3 us (90%)
  local copies, waits for them, and re-layouts  2 us (7%)
  between operations  0.65 us (2%)
    pallas_call x1, Pallas kernels, on_device(): pl.pallas_call(functools.partial(kernel, layers, n), out_shape=(jax.Shape...  24.3 us
    unnamed x4, local copies, waits for them, and re-layouts  2 us

profile of v5, /device:TPU:8, one launch (start us, length us, event | category | flops | bytes accessed | tf_op | source)
XLA Modules:
  0.0 26.9 jit_solution(5777588472949249098)
XLA Ops:
  0.6 24.3 %shard_map.77 = (bf16[1,2,32,256]{3,2,1,0:T(8,128)(2,1)}, bf16[1,2,32,256]{3,2,1,0:T(8,128)(2,1)}) custom-call(bf16[1,2,32,256]{3,2,1,0:T(8,128)(2,1)} %up_hbm.1, bf16[1,2,32,256]{3,2,1,0:T(8,128)(2,1)} %down_hbm.1, s32[1,32]{1,0:T(1,128)} %bitcast.1, bf16[1,1,4,2,128,256]{5,4,3,2,1,0:T(8,128)(2,1)} %u_hbm.1, bf16[1,1,4,2,128,256]{5,4,3,2,1,0:T(8,128)(2,1)} %v_hbm.1, ...), custom_call_target="tpu_custom_call" | custom-call | tf_op jit(solution)/shard_map/pallas_call | solution.py:328
  24.9 0.0 copy-start
  24.9 1.4 %copy.10 = bf16[1,2,32,256]{3,2,1,0:T(8,128)(2,1)} copy(bf16[1,2,32,256]{3,2,1,0:T(8,128)(2,1)} %get-tuple-element.4) | data formatting | bytes 65536
  26.3 0.0 copy-done
  26.3 0.6 %copy.11 = bf16[1,2,32,256]{3,2,1,0:T(8,128)(2,1)} copy(bf16[1,2,32,256]{3,2,1,0:T(8,128)(2,1)S(1)} %copy-done) | data formatting | bytes 65536
Async XLA Ops:
  24.9 1.4 %copy-start = (bf16[1,2,32,256]{3,2,1,0:T(8,128)(2,1)S(1)}, bf16[1,2,32,256]{3,2,1,0:T(8,128)(2,1)}, u32[]{:S(2)}) copy-start(bf16[1,2,32,256]{3,2,1,0:T(8,128)(2,1)} %get-tuple-element.5) | copy-start | bytes 98308

commit v6 on v5

--- a/solution.py
+++ b/solution.py
@@ -315,6 +315,19 @@
     put_up.wait()
 
 
+def hand_over(up_ref, down_ref, up_out, down_out, up_mem, down_mem, sems):
+    pairs = [(up_ref, up_mem, up_out), (down_ref, down_mem, down_out)]
+    loads = [pltpu.make_async_copy(src, mem, sems.at[0, i]) for i, (src, mem, _) in enumerate(pairs)]
+    stores = [pltpu.make_async_copy(mem, dst, sems.at[1, i]) for i, (_, mem, dst) in enumerate(pairs)]
+    for load in loads:
+        load.start()
+    for load, store in zip(loads, stores):
+        load.wait()
+        store.start()
+    for store in stores:
+        store.wait()
+
+
 def solution(mesh):
     layers, n = mesh.shape["gz"], mesh.shape["xy"]
 
@@ -325,7 +338,7 @@
         anywhere = pl.BlockSpec(memory_space=pl.ANY)
         hbm = pl.BlockSpec(memory_space=pltpu.HBM)
         dma = pltpu.SemaphoreType.DMA
-        return pl.pallas_call(
+        traces = pl.pallas_call(
             functools.partial(kernel, layers, n),
             out_shape=(
                 jax.ShapeDtypeStruct(up_source.shape, jnp.bfloat16),
@@ -374,6 +387,20 @@
                 collective_id=0, has_side_effects=True
             ),
         )(up_source, down_source, source_layer.reshape(1, sources), u_factor, v_factor, block_rank)
+        return pl.pallas_call(
+            hand_over,
+            out_shape=(
+                jax.ShapeDtypeStruct(up_source.shape, jnp.bfloat16),
+                jax.ShapeDtypeStruct(down_source.shape, jnp.bfloat16),
+            ),
+            in_specs=[anywhere, anywhere],
+            out_specs=(anywhere, anywhere),
+            scratch_shapes=[
+                pltpu.VMEM(up_source.shape, jnp.bfloat16),
+                pltpu.VMEM(down_source.shape, jnp.bfloat16),
+                dma((2, 2)),
+            ],
+        )(*traces)
 
     in_specs = (
         P("gz", None, None, "xy"),

time: 27.1 us -> 26.6 us (0.982)
  local copies, waits for them, and re-layouts: 2 us -> 0 us
  Pallas kernels: 24.3 us -> 25.7 us
    unnamed x4 -> x0, local copies, waits for them, and re-layouts: 2 us -> none
    pallas_call x0 -> x1, Pallas kernels: none -> 1.42 us  [on_device(): pl.pallas_call(hand_over, out_shape=(jax.ShapeDtypeStruct(up_source.shape...]
where the time goes in v6:
time: 26.6 us; the launch traced here: 26.3 us
  Pallas kernels  25.7 us (97%)
  between operations  0.64 us (2%)
    pallas_call x1, Pallas kernels, on_device(): pl.pallas_call(functools.partial(kernel, layers, n), out_shape=(jax.Shape...  24.3 us
    pallas_call x1, Pallas kernels, on_device(): pl.pallas_call(hand_over, out_shape=(jax.ShapeDtypeStruct(up_source.shape...  1.42 us

profile of v6, /device:TPU:8, one launch (start us, length us, event | category | flops | bytes accessed | tf_op | source)
XLA Modules:
  0.0 26.3 jit_solution(12720733570034399094)
XLA Ops:
  0.6 24.3 %shard_map.77 = (bf16[1,2,32,256]{3,2,1,0:T(8,128)(2,1)}, bf16[1,2,32,256]{3,2,1,0:T(8,128)(2,1)}) custom-call(bf16[1,2,32,256]{3,2,1,0:T(8,128)(2,1)} %up_hbm.1, bf16[1,2,32,256]{3,2,1,0:T(8,128)(2,1)} %down_hbm.1, s32[1,32]{1,0:T(1,128)} %bitcast.1, bf16[1,1,4,2,128,256]{5,4,3,2,1,0:T(8,128)(2,1)} %u_hbm.1, bf16[1,1,4,2,128,256]{5,4,3,2,1,0:T(8,128)(2,1)} %v_hbm.1, ...), custom_call_target="tpu_custom_call" | custom-call | tf_op jit(solution)/shard_map/pallas_call | solution.py:341
  24.9 1.4 %shard_map.78 = (bf16[1,2,32,256]{3,2,1,0:T(8,128)(2,1)}, bf16[1,2,32,256]{3,2,1,0:T(8,128)(2,1)}) custom-call(bf16[1,2,32,256]{3,2,1,0:T(8,128)(2,1)} %get-tuple-element.4.up_ref, bf16[1,2,32,256]{3,2,1,0:T(8,128)(2,1)} %get-tuple-element.5.down_ref), custom_call_target="tpu_custom_call" | custom-call | tf_op jit(solution)/shard_map/pallas_call | solution.py:390

commit v7 on v6

--- a/solution.py
+++ b/solution.py
@@ -146,7 +146,8 @@
     def arrived(ref, rsem):
         remote(ref, ref, next_ssem, rsem, layer, me).wait_recv()
 
-    for k in range(1, n):
+    far_first = [*range(2, n), 1]
+    for k in far_first:
         gather(k).start()
 
     @pl.when(has_below)
@@ -196,7 +197,7 @@
 
             @pl.when(has_below)
             def _():
-                for k in range(n // 2):
+                for k in reversed(range(n // 2)):
                     wait_blocks(t, [like[k]])
                     relay(t, k).start()
 
@@ -217,7 +218,7 @@
             down = total.astype(jnp.bfloat16)
 
         if last:
-            for k in range(1, n):
+            for k in far_first:
                 last_send[k] = piece(others[k]).astype(jnp.bfloat16)
                 last_part(k).start()
         else:

time: 26.6 us -> 26.6 us (level)
  no operation moved by 1% of the time
where the time goes in v7:
time: 26.6 us; the launch traced here: 26.3 us
  Pallas kernels  25.7 us (97%)
  between operations  0.64 us (2%)
    pallas_call x1, Pallas kernels, on_device(): pl.pallas_call(functools.partial(kernel, layers, n), out_shape=(jax.Shape...  24.3 us
    pallas_call x1, Pallas kernels, on_device(): pl.pallas_call(hand_over, out_shape=(jax.ShapeDtypeStruct(up_source.shape...  1.42 us

profile of v7, /device:TPU:8, one launch (start us, length us, event | category | flops | bytes accessed | tf_op | source)
XLA Modules:
  0.0 26.3 jit_solution(17076548757866172997)
XLA Ops:
  0.6 24.3 %shard_map.77 = (bf16[1,2,32,256]{3,2,1,0:T(8,128)(2,1)}, bf16[1,2,32,256]{3,2,1,0:T(8,128)(2,1)}) custom-call(bf16[1,2,32,256]{3,2,1,0:T(8,128)(2,1)} %up_hbm.1, bf16[1,2,32,256]{3,2,1,0:T(8,128)(2,1)} %down_hbm.1, s32[1,32]{1,0:T(1,128)} %bitcast.1, bf16[1,1,4,2,128,256]{5,4,3,2,1,0:T(8,128)(2,1)} %u_hbm.1, bf16[1,1,4,2,128,256]{5,4,3,2,1,0:T(8,128)(2,1)} %v_hbm.1, ...), custom_call_target="tpu_custom_call" | custom-call | tf_op jit(solution)/shard_map/pallas_call | solution.py:342
  24.9 1.4 %shard_map.78 = (bf16[1,2,32,256]{3,2,1,0:T(8,128)(2,1)}, bf16[1,2,32,256]{3,2,1,0:T(8,128)(2,1)}) custom-call(bf16[1,2,32,256]{3,2,1,0:T(8,128)(2,1)} %get-tuple-element.4.up_ref, bf16[1,2,32,256]{3,2,1,0:T(8,128)(2,1)} %get-tuple-element.5.down_ref), custom_call_target="tpu_custom_call" | custom-call | tf_op jit(solution)/shard_map/pallas_call | solution.py:391
